TPU v7x, 32 devices: a whole 2x2x4 slice. The times are simulated.
32 devices in a mesh: freq: 8 (over z, core), mode: 4 (over y, x).
Axes of the slice: x: 2, y: 2, z: 4, core: 2. Of those that a mesh axis runs over, the one named last changes fastest.
Arguments:
- sources: bfloat16 [16, 512, 2, 4096], P(None, None, None, ('freq', 'mode')), may hold values from -6 to 6
- mapping: bfloat16 [16, 2, 2048, 4096], P('freq', None, 'mode'), may hold values from -0.0625 to 0.0625
Outputs:
- pressure: bfloat16 [16, 512, 2, 2048], P(None, 'freq', None, 'mode')
All inputs are finite; a program needn't handle non-finite values.
Results may differ from a plain program's by a relative error of at most 0.0006.
Values may be sent and summed in bfloat16 or wider, within the bound.
A program may use at most 128 MiB of HBM per device.

v0:
```python
import jax
import jax.numpy as jnp
from jax import lax
from jax.sharding import PartitionSpec as P


def body(sources, mapping):
    freq_count = lax.axis_size("freq")
    mode_count = lax.axis_size("mode")
    bin_count = mapping.shape[0]
    slice_width = sources.shape[3]
    regrouped = lax.all_to_all(sources, "freq", split_axis=0, concat_axis=3, tiled=True)
    snapshots = regrouped.shape[1]
    blocked = regrouped.reshape(bin_count, snapshots, 2, 1, freq_count, slice_width)
    gathered = lax.all_gather(blocked, "mode", axis=3, tiled=True)
    complete = jnp.swapaxes(gathered, 3, 4).reshape(bin_count, snapshots, 2, -1)
    real_part = jnp.einsum(
        "bsm,bom->bso", complete[:, :, 0], mapping[:, 0], preferred_element_type=jnp.float32
    ) - jnp.einsum(
        "bsm,bom->bso", complete[:, :, 1], mapping[:, 1], preferred_element_type=jnp.float32
    )
    imag_part = jnp.einsum(
        "bsm,bom->bso", complete[:, :, 1], mapping[:, 0], preferred_element_type=jnp.float32
    ) + jnp.einsum(
        "bsm,bom->bso", complete[:, :, 0], mapping[:, 1], preferred_element_type=jnp.float32
    )
    field = jnp.stack([real_part, imag_part], axis=2)
    bins_total = bin_count * freq_count
    first_bin = lax.axis_index("freq") * bin_count
    bin_index = (first_bin + jnp.arange(bin_count, dtype=jnp.int32)).astype(jnp.float32)
    weights = ((bin_index + 1.0) / bins_total) ** 2
    local_energy = jnp.sum(weights[:, None, None, None] * field * field)
    energy = lax.psum(local_energy, ("freq", "mode"))
    energy = energy / (field.shape[1] * field.shape[3] * mode_count)
    factor = jnp.sqrt(bins_total / (energy + 1e-06))
    result = lax.all_to_all(
        (field * factor).astype(jnp.bfloat16), "freq", split_axis=1, concat_axis=0, tiled=True
    )
    return result


def solution(mesh):
    placed = (P(None, None, None, ("freq", "mode")), P("freq", None, "mode", None))
    return jax.shard_map(
        body, mesh=mesh, in_specs=placed, out_specs=P(None, "freq", None, "mode"), check_vma=False
    )
```

profile of v0, /device:TPU:9, one launch (start us, length us, event | category | flops | bytes accessed | tf_op | source)
XLA Modules:
  0.0 469.6 jit_solution(15611076914805232381)
XLA Ops:
  6.5 0.0 all-gather.3.cloned.1.call-start
  6.5 3.2 copy.16
  9.7 96.5 %all_to_all.33 = bf16[16,512,2,128]{3,1,2,0:T(8,128)(2,1)} all-to-all(bf16[16,512,2,128]{3,1,2,0:T(8,128)(2,1)S(1)} %copy.16), channel_id=1, replica_groups=mesh['freq'=8,'mode'=4] {'freq'}, dimensions={0} | all-to-all | bytes 8388608 | tf_op jit(solution)/shard_map/all_to_all | solution.py:12
  106.2 0.0 all-gather.3.cloned.1.call-update
  106.3 158.4 %all-gather.3.cloned.1.call-done = bf16[2,512,2,32,128]{4,1,2,0,3:T(8,128)(2,1)} async-done(((bf16[2,512,2,8,128]{4,1,2,0,3:T(8,128)(2,1)}), bf16[2,512,2,32,128]{4,1,2,0,3:T(8,128)(2,1)}) %all-gather.3.cloned.1.call-update) | async-done | bytes 16777232 | tf_op jit(solution)/shard_map/all_gather | solution.py:15
  264.6 22.3 %copy.18 = bf16[2,512,2,8,4,128]{5,4,3,1,0,2:T(4,128)(2,1)} copy(bf16[2,512,2,8,4,128]{5,1,2,0,3,4:T(8,128)(2,1)} %bitcast.46) | data formatting | bytes 33554432 | tf_op jit(solution)/shard_map/transpose | solution.py:16
  286.9 27.7 %reshape.16 = bf16[2,512,2,4096]{3,1,0,2:T(8,128)(2,1)} reshape(bf16[2,512,2,8,4,128]{5,4,3,1,0,2:T(4,128)(2,1)} %copy.18) | data formatting | bytes 33554432 | tf_op jit(solution)/shard_map/reshape | solution.py:16
  314.6 11.6 %fusion.2 = f32[2,512,512]{2,1,0:T(8,128)} fusion(bf16[2,512,2,4096]{3,1,0,2:T(8,128)(2,1)} %reshape.16, bf16[2,2,512,4096]{3,2,1,0:T(8,128)(2,1)} %param.3), kind=kOutput, calls=%fused_computation.4 | convolution fusion | flops 4294967296 | bytes 18874368 | tf_op jit(solution)/shard_map/bsm,bom->bso/dot_general | solution.py:19
  326.2 11.6 %fusion = f32[2,512,512]{2,1,0:T(8,128)} fusion(bf16[2,512,2,4096]{3,1,0,2:T(8,128)(2,1)} %reshape.16, bf16[2,2,512,4096]{3,2,1,0:T(8,128)(2,1)} %param.3), kind=kOutput, calls=%fused_computation.2 | convolution fusion | flops 4294967296 | bytes 18874368 | tf_op jit(solution)/shard_map/bsm,bom->bso/dot_general | solution.py:24
  337.8 10.9 %subtract_bitcast_fusion = f32[2,512,1,512]{3,1,0,2:T(8,128)S(1)} fusion(f32[2,512,512]{2,1,0:T(8,128)} %fusion.2, bf16[2,2,512,4096]{3,2,1,0:T(8,128)(2,1)} %param.3, bf16[2,512,2,4096]{3,1,0,2:T(8,128)(2,1)} %reshape.16), kind=kOutput, calls=%fused_computation.19 | convolution fusion | flops 4295491584 | bytes 20971520 | tf_op jit(solution)/shard_map/bsm,bom->bso/dot_general | solution.py:17
  348.7 12.4 %add_bitcast_fusion = f32[2,512,1,512]{3,1,0,2:T(8,128)} fusion(f32[2,512,512]{2,1,0:T(8,128)} %fusion, bf16[2,2,512,4096]{3,2,1,0:T(8,128)(2,1)} %param.3, bf16[2,512,2,4096]{3,1,0,2:T(8,128)(2,1)} %reshape.16), kind=kOutput, calls=%fused_computation.18 | convolution fusion | flops 4295491584 | bytes 20971520 | tf_op jit(solution)/shard_map/bsm,bom->bso/dot_general | solution.py:22
  361.2 3.4 fusion.12
  364.6 39.1 %psum.7 = f32[]{:T(128)} all-reduce(f32[]{:T(128)} %fusion.12), channel_id=1, replica_groups=mesh['freq'=8,'mode'=4] {'freq','mode'}, use_global_device_ids=true, to_apply=%region_1.0 | all-reduce | flops 1 | bytes 8 | tf_op jit(solution)/shard_map/psum | solution.py:33
  404.5 2.2 multiply_convert_fusion
  406.6 2.2 copy.21
  408.8 50.8 %all_to_all.34 = bf16[2,512,2,512]{3,0,2,1:T(2,128)(2,1)S(1)} all-to-all(bf16[2,512,2,512]{3,0,2,1:T(2,128)(2,1)S(1)} %copy.21), channel_id=1, replica_groups=mesh['freq'=8,'mode'=4] {'freq'}, dimensions={1} | all-to-all | bytes 4194304 | tf_op jit(solution)/shard_map/all_to_all | solution.py:36
  459.6 3.2 copy.22
  (1 shorter events, 0.0 us)
Async XLA Ops:
  6.5 258.1 %all-gather.3.cloned.1.call-start = ((), (), s32[]{:S(2)}) async-start(), calls=%async_computation.2 | async-start | bytes 20971520 | tf_op jit(solution)/shard_map/all_gather | solution.py:15
Sparse Core Ops, SparseCore 0:
  106.4 158.2 all-gather.2
where the time goes:
time: 474 us; the launch traced here: 470 us
  blocking collectives  186 us (39%)
  waiting for transfers between devices  158 us (33%)
  local copies, waits for them, and re-layouts  58.5 us (12%)
  matrix products  46.6 us (10%)
  between operations  14.2 us (3%)
  other arithmetic  5.6 us (1%)
    all_gather x1, waiting for transfers between devices, body(): gathered = lax.all_gather(blocked, 'mode', axis=3, tiled=True)  158 us
    all_to_all x1, blocking collectives, body(): lax.all_to_all(sources, 'freq', split_axis=0, concat_axis=3, tiled=True)  96.5 us
    all_to_all x1, blocking collectives, body(): lax.all_to_all((field * factor).astype(jnp.bfloat16), 'freq', split_axis=...  50.8 us
    psum x1, blocking collectives, body(): energy = lax.psum(local_energy, ('freq', 'mode'))  39.1 us
    reshape x1, local copies, waits for them, and re-layouts, body(): complete = jnp.swapaxes(gathered, 3, 4).reshape(bin_count, snapshots, 2, -1)  27.7 us
    transpose x1, local copies, waits for them, and re-layouts, body(): complete = jnp.swapaxes(gathered, 3, 4).reshape(bin_count, snapshots, 2, -1)  22.3 us
    dot_general x1, matrix products, body(): jnp.einsum('bsm,bom->bso', complete[:, :, 1], mapping[:, 0], preferred_el...  12.4 us
    dot_general x1, matrix products, body(): jnp.einsum('bsm,bom->bso', complete[:, :, 1], mapping[:, 1], preferred_el...  11.6 us
  transfers between devices with their start and end apart: 1, of which 1 were waited for; matrix products, arithmetic and copies ran while one was open for 0% of the time, Pallas kernels for 0%

commit v1 on v0

--- a/solution.py
+++ b/solution.py
@@ -1,10 +1,18 @@
+import functools
+
 import jax
 import jax.numpy as jnp
 from jax import lax
+from jax.experimental import pallas as pl
+from jax.experimental.pallas import tpu as pltpu
 from jax.sharding import PartitionSpec as P
 
-
-def body(sources, mapping):
+MESH = pl.DeviceIdType.MESH
+LANES = 128
+AHEAD = 3
+
+
+def plain_body(sources, mapping):
     freq_count = lax.axis_size("freq")
     mode_count = lax.axis_size("mode")
     bin_count = mapping.shape[0]
@@ -39,6 +47,251 @@
     return result
 
 
+def kernel(
+    dims, src, mapping, out, held, maps, field, ready, power, by_freq, by_mode,
+    map_sem, own_sem, z_send, z_recv, x_send, x_recv, y_send, y_recv,
+    fx_send, fx_recv, fy_send, fy_recv, ef_send, ef_recv, em_send, em_recv,
+    o_own, o_send, o_recv,
+):
+    F, M, B, R, O = dims
+    half = F // 2
+    f = lax.axis_index("freq")
+    m = lax.axis_index("mode")
+    mx = m + 1 - 2 * lax.rem(m, 2)
+    my = lax.rem(m + 2, 4)
+
+    def freq_peer(step):
+        return lax.rem(f + step, F)
+
+    def mode_peer(step):
+        return lax.rem(m + step, M)
+
+    for b in range(B):
+        for c in range(2):
+            pltpu.make_async_copy(mapping.at[b, c], maps.at[b, c], map_sem.at[b, c]).start()
+
+    def own_copy(k):
+        return pltpu.make_async_copy(
+            src.at[pl.ds(f * B, B), pl.ds(k * R, R)], held.at[k, m, f], own_sem.at[k]
+        )
+
+    def own_start(k, carry):
+        own_copy(k).start()
+        return carry
+
+    lax.fori_loop(0, F, own_start, 0)
+
+    barrier = pltpu.get_barrier_semaphore()
+    for step in range(1, F):
+        pl.semaphore_signal(barrier, inc=1, device_id=(freq_peer(step), m), device_id_type=MESH)
+    for step in range(1, M):
+        pl.semaphore_signal(barrier, inc=1, device_id=(f, mode_peer(step)), device_id_type=MESH)
+    pl.semaphore_wait(barrier, F + M - 2)
+
+    def z_start(k):
+        for step in range(1, F):
+            there = freq_peer(step)
+            pltpu.make_async_remote_copy(
+                src_ref=src.at[pl.ds(there * B, B), pl.ds(k * R, R)],
+                dst_ref=held.at[k, m, f],
+                send_sem=z_send.at[k],
+                recv_sem=z_recv.at[k],
+                device_id=(there, m),
+                device_id_type=MESH,
+            ).start()
+
+    def z_wait(sem, k):
+        peers = held.at[k, m, pl.ds(0, F - 1)]
+        pltpu.make_async_copy(peers, peers, sem.at[k]).wait()
+
+    def spread(k, to, send, recv):
+        return pltpu.make_async_remote_copy(
+            src_ref=held.at[k, m], dst_ref=held.at[k, m],
+            send_sem=send.at[k], recv_sem=recv.at[k],
+            device_id=(f, to), device_id_type=MESH,
+        )
+
+    def relay(k, whose, first, to, send, recv):
+        part = held.at[k, whose, pl.ds(first, half)]
+        return pltpu.make_async_remote_copy(
+            src_ref=part, dst_ref=part,
+            send_sem=send.at[k], recv_sem=recv.at[k],
+            device_id=(f, to), device_id_type=MESH,
+        )
+
+    def compute(k):
+        def one_bin(b, carry):
+            direct = None
+            for g in range(F):
+                lhs = jnp.concatenate([held[k, j, g, b] for j in range(M)], axis=1)
+                cols = pl.ds(g * M * LANES, M * LANES)
+                nt = (((1,), (1,)), ((), ()))
+                p = lax.dot_general(lhs, maps[b, 0, :, cols], nt, preferred_element_type=jnp.float32)
+                q = lax.dot_general(lhs, maps[b, 1, :, cols], nt, preferred_element_type=jnp.float32)
+                direct = p if direct is None else direct + p
+                cross = q if g == 0 else cross + q
+            even = lax.rem(lax.broadcasted_iota(jnp.int32, (R, O), 0), 2) == 0
+            turned = jnp.where(even, -pltpu.roll(cross, R - 1, 0), pltpu.roll(cross, 1, 0))
+            value = direct + turned
+            field[k, b] = value
+            root = (f * B + b + 1).astype(jnp.float32) / (B * F)
+            squares = jnp.sum((value * value).reshape(R // 8, 8, O), axis=0)
+            folded = squares[:, :LANES]
+            for j in range(1, O // LANES):
+                folded = folded + squares[:, j * LANES : (j + 1) * LANES]
+            power[...] += folded * (root * root)
+            return carry
+
+        lax.fori_loop(0, B, one_bin, 0)
+
+    power[...] = jnp.zeros_like(power)
+    for k in range(min(AHEAD, F)):
+        z_start(k)
+
+    def step_fn(k, carry):
+        @pl.when(k < F)
+        def _():
+            own_copy(k).wait()
+            z_wait(z_recv, k)
+            spread(k, mx, x_send, x_recv).start()
+            spread(k, my, y_send, y_recv).start()
+
+        @pl.when(k + AHEAD < F)
+        def _():
+            z_start(k + AHEAD)
+
+        @pl.when((k >= 1) & (k <= F))
+        def _():
+            last = k - 1
+            spread(last, mx, x_send, x_recv).wait_recv()
+            relay(last, mx, 0, my, fy_send, fy_recv).start()
+            spread(last, my, y_send, y_recv).wait_recv()
+            relay(last, my, half, mx, fx_send, fx_recv).start()
+
+        @pl.when(k == 2)
+        def _():
+            for b in range(B):
+                for c in range(2):
+                    pltpu.make_async_copy(mapping.at[b, c], maps.at[b, c], map_sem.at[b, c]).wait()
+
+        @pl.when(k >= 2)
+        def _():
+            done = k - 2
+            relay(done, mx, 0, my, fy_send, fy_recv).wait_recv()
+            relay(done, my, half, mx, fx_send, fx_recv).wait_recv()
+            compute(done)
+
+        return carry
+
+    lax.fori_loop(0, F + 2, step_fn, 0)
+
+    by_freq[f] = power[...]
+    for step in range(1, F):
+        pltpu.make_async_remote_copy(
+            src_ref=power, dst_ref=by_freq.at[f], send_sem=ef_send, recv_sem=ef_recv,
+            device_id=(freq_peer(step), m), device_id_type=MESH,
+        ).start()
+    peers = by_freq.at[pl.ds(0, F - 1)]
+    pltpu.make_async_copy(peers, peers, ef_recv).wait()
+    pltpu.make_async_copy(peers, peers, ef_send).wait()
+    power[...] = jnp.sum(by_freq[...], axis=0)
+    by_mode[m] = power[...]
+    for step in range(1, M):
+        pltpu.make_async_remote_copy(
+            src_ref=power, dst_ref=by_mode.at[m], send_sem=em_send, recv_sem=em_recv,
+            device_id=(f, mode_peer(step)), device_id_type=MESH,
+        ).start()
+    peers = by_mode.at[pl.ds(0, M - 1)]
+    pltpu.make_async_copy(peers, peers, em_recv).wait()
+    pltpu.make_async_copy(peers, peers, em_send).wait()
+    energy = jnp.sum(jnp.sum(by_mode[...], axis=0), keepdims=True) / (F * (R // 2) * O * M)
+    factor = jnp.sqrt(B * F / (energy + 1e-06))
+
+    def scale(k):
+        for b in range(B):
+            for j in range(O // LANES):
+                piece = field[k, b, :, j * LANES : (j + 1) * LANES] * factor
+                ready[k, b, j] = piece.astype(jnp.bfloat16)
+
+    def finish(step, carry):
+        there = freq_peer(step)
+        scale(there)
+        pltpu.make_async_remote_copy(
+            src_ref=ready.at[there], dst_ref=out.at[pl.ds(f * B, B)],
+            send_sem=o_send, recv_sem=o_recv,
+            device_id=(there, m), device_id_type=MESH,
+        ).start()
+        return carry
+
+    lax.fori_loop(1, F, finish, 0)
+    scale(f)
+    mine = pltpu.make_async_copy(ready.at[f], out.at[pl.ds(f * B, B)], o_own)
+    mine.start()
+
+    def drain(k, carry):
+        z_wait(z_send, k)
+        spread(k, mx, x_send, x_recv).wait_send()
+        spread(k, my, y_send, y_recv).wait_send()
+        relay(k, mx, 0, my, fy_send, fy_recv).wait_send()
+        relay(k, my, half, mx, fx_send, fx_recv).wait_send()
+        return carry
+
+    lax.fori_loop(0, F, drain, 0)
+    mine.wait()
+    peers = ready.at[pl.ds(0, F - 1)]
+    pltpu.make_async_copy(peers, peers, o_send).wait()
+    pltpu.make_async_copy(peers, peers, o_recv).wait()
+
+
+def kernel_body(sources, mapping):
+    F = lax.axis_size("freq")
+    M = lax.axis_size("mode")
+    bins, snaps = sources.shape[:2]
+    B, _, O, modes = mapping.shape
+    R = 2 * snaps // F
+    dma = pltpu.SemaphoreType.DMA
+    any_space = pl.BlockSpec(memory_space=pl.ANY)
+    out = pl.pallas_call(
+        functools.partial(kernel, (F, M, B, R, O)),
+        out_shape=jax.ShapeDtypeStruct((bins, O // LANES, R, LANES), jnp.bfloat16),
+        in_specs=[any_space, any_space],
+        out_specs=any_space,
+        scratch_shapes=[
+            pltpu.VMEM((F, M, F, B, R, LANES), jnp.bfloat16),
+            pltpu.VMEM((B, 2, O, modes), jnp.bfloat16),
+            pltpu.VMEM((F, B, R, O), jnp.float32),
+            pltpu.VMEM((F, B, O // LANES, R, LANES), jnp.bfloat16),
+            pltpu.VMEM((8, LANES), jnp.float32),
+            pltpu.VMEM((F, 8, LANES), jnp.float32),
+            pltpu.VMEM((M, 8, LANES), jnp.float32),
+            dma((B, 2)),
+            dma((F,)),
+        ]
+        + [dma((F,))] * 10
+        + [dma(())] * 7,
+        compiler_params=pltpu.CompilerParams(
+            collective_id=0, has_side_effects=True, vmem_limit_bytes=62 * 1024 * 1024
+        ),
+    )(sources.reshape(bins, 2 * snaps, LANES), mapping)
+    out = out.reshape(bins, O // LANES, R // 2, 2, LANES)
+    return jnp.transpose(out, (0, 2, 3, 1, 4)).reshape(bins, R // 2, 2, O)
+
+
+def body(sources, mapping):
+    freq_count = lax.axis_size("freq")
+    snaps, width = sources.shape[1], sources.shape[3]
+    held = 2 * mapping.size + 2 * mapping.shape[0] * snaps * 2 * mapping.shape[3]
+    fits = (
+        lax.axis_size("mode") == 4
+        and freq_count % 2 == 0
+        and width == LANES
+        and mapping.shape[2] % LANES == 0
+        and snaps % (8 * freq_count) == 0
+        and held <= 40 * 1024 * 1024
+    )
+    return (kernel_body if fits else plain_body)(sources, mapping)
+
+
 def solution(mesh):
     placed = (P(None, None, None, ("freq", "mode")), P("freq", None, "mode", None))
     return jax.shard_map(

time: 474 us -> 229 us (0.48)
  Pallas kernels: 0 us -> 224 us
  blocking collectives: 186 us -> 0 us
  waiting for transfers between devices: 158 us -> 0 us
  local copies, waits for them, and re-layouts: 58.5 us -> 4.46 us
  matrix products: 46.6 us -> 0 us
  between operations: 14.2 us -> 0.01 us
  other arithmetic: 5.6 us -> 0 us
    pallas_call x0 -> x1, Pallas kernels: none -> 224 us  [kernel_body(): pl.pallas_call(functools.partial(kernel, (F, M, B, R, O)), out_shape=jax....]
    all_gather x1 -> x0, waiting for transfers between devices: 158 us -> none  [body(): gathered = lax.all_gather(blocked, 'mode', axis=3, tiled=True)]
    all_to_all x2 -> x0, blocking collectives: 147 us -> none  [the longest x1 96.5 us: body(): lax.all_to_all(sources, 'freq', split_axis=0, concat_axis=3, tiled=True)]
    dot_general x4 -> x0, matrix products: 46.6 us -> none  [the longest x1 12.4 us: body(): jnp.einsum('bsm,bom->bso', complete[:, :, 1], mapping[:, 0], preferred_el...]
    psum x1 -> x0, blocking collectives: 39.1 us -> none  [body(): energy = lax.psum(local_energy, ('freq', 'mode'))]
    reshape x1, local copies, waits for them, and re-layouts: 27.7 us -> 4.46 us  [kernel_body(): return jnp.transpose(out, (0, 2, 3, 1, 4)).reshape(bins, R // 2, 2, O)]
    transpose x1 -> x0, local copies, waits for them, and re-layouts: 22.3 us -> none  [body(): complete = jnp.swapaxes(gathered, 3, 4).reshape(bin_count, snapshots, 2, -1)]
  transfers between devices with their start and end apart: 1 -> 0, of which waited for: 1 -> 0; matrix products, arithmetic and copies ran while one was open for 0% -> 0% of each run, Pallas kernels for 0% -> 0%
where the time goes in v1:
time: 229 us
  Pallas kernels  224 us (98%)
  local copies, waits for them, and re-layouts  4.46 us (2%)
    pallas_call x1, Pallas kernels, kernel_body(): pl.pallas_call(functools.partial(kernel, (F, M, B, R, O)), out_shape=jax....  224 us

profile of v1, /device:TPU:9, one launch (start us, length us, event | category | flops | bytes accessed | tf_op | source)
XLA Modules:
  0.0 228.8 jit_solution(6885030051657564535)
XLA Ops:
  0.0 224.3 %shard_map.28 = bf16[16,4,128,128]{3,2,1,0:T(8,128)(2,1)} custom-call(bf16[16,1024,128]{2,1,0:T(8,128)(2,1)} %bitcast.9, bf16[2,2,512,4096]{3,2,1,0:T(8,128)(2,1)} %mapping.1), custom_call_target="tpu_custom_call" | custom-call | tf_op jit(solution)/shard_map/pallas_call | solution.py:254
  224.3 4.5 %copy.6 = bf16[16,4,64,1,2,128]{5,4,1,3,2,0:T(2,128)(2,1)} copy(bf16[16,4,64,1,2,128]{5,4,3,2,1,0:T(2,128)(2,1)} %bitcast.8) | data formatting | bytes 4194304 | tf_op jit(solution)/shard_map/reshape | solution.py:277

commit v2 on v0

--- a/solution.py
+++ b/solution.py
@@ -1,10 +1,20 @@
+import functools
+
 import jax
 import jax.numpy as jnp
 from jax import lax
+from jax.experimental import pallas as pl
+from jax.experimental.pallas import tpu as pltpu
 from jax.sharding import PartitionSpec as P
 
-
-def body(sources, mapping):
+MESH = pl.DeviceIdType.MESH
+LANES = 128
+AHEAD = 3
+ROWS = 16
+EARLY = 5
+
+
+def plain_body(sources, mapping):
     freq_count = lax.axis_size("freq")
     mode_count = lax.axis_size("mode")
     bin_count = mapping.shape[0]
@@ -39,6 +49,329 @@
     return result
 
 
+def kernel(
+    dims, src, mapping, out, held, maps, field, early, ready, scaled, power, by_mode, by_freq,
+    map_sem, own_sem, z_send, z_recv, x_send, x_recv, y_send, y_recv,
+    fx_send, fx_recv, fy_send, fy_recv, e_send, e_recv,
+    ox_send, ox_recv, oy_send, oy_recv, of_send, of_recv,
+    em_send, em_recv, ef_send, ef_recv, o_own, o_send, o_recv,
+):
+    F, M, B, K, C, O, E = dims
+    R = F * C
+    cut = F // 2
+    f = lax.axis_index("freq")
+    m = lax.axis_index("mode")
+    mx = m + 1 - 2 * lax.rem(m, 2)
+    my = lax.rem(m + 2, 4)
+    md = lax.rem(mx + 2, 4)
+
+    def freq_peer(step):
+        return lax.rem(f + step, F)
+
+    def mode_peer(step):
+        return lax.rem(m + step, M)
+
+    def remote(src_ref, dst_ref, send, recv, to_f, to_m):
+        return pltpu.make_async_remote_copy(
+            src_ref=src_ref, dst_ref=dst_ref, send_sem=send, recv_sem=recv,
+            device_id=(to_f, to_m), device_id_type=MESH,
+        )
+
+    def await_bytes(ref, sem):
+        pltpu.make_async_copy(ref, ref, sem).wait()
+
+    def chunk(owner, k):
+        return src.at[pl.ds(owner * B, B), :, pl.ds(pl.multiple_of(k * C, C), C)]
+
+    def own_copy(k):
+        return pltpu.make_async_copy(chunk(f, k), held.at[k, m, 0], own_sem.at[k])
+
+    barrier = pltpu.get_barrier_semaphore()
+    for step in range(1, F):
+        pl.semaphore_signal(barrier, inc=1, device_id=(freq_peer(step), m), device_id_type=MESH)
+    for step in range(1, M):
+        pl.semaphore_signal(barrier, inc=1, device_id=(f, mode_peer(step)), device_id_type=MESH)
+    pl.semaphore_wait(barrier, F + M - 2)
+
+    def z_start(k):
+        for step in range(1, F):
+            there = freq_peer(step)
+            remote(
+                chunk(there, k), held.at[k, m, F - step], z_send.at[k], z_recv.at[k], there, m
+            ).start()
+
+    def z_slots(k):
+        return held.at[k, m, pl.ds(1, F - 1)]
+
+    def spread(k, whose, to, send, recv):
+        part = held.at[k, whose, pl.ds(1, F - 1)]
+        return remote(part, part, send.at[k], recv.at[k], f, to)
+
+    def relay_y(k):
+        part = held.at[k, mx, pl.ds(1, cut - 1)]
+        return remote(part, part, fy_send.at[k], fy_recv.at[k], f, my)
+
+    def relay_x(k):
+        part = held.at[k, my, pl.ds(cut, F - cut)]
+        return remote(part, part, fx_send.at[k], fx_recv.at[k], f, mx)
+
+    def own_slots(whose):
+        return held.at[pl.ds(0, K), whose, 0]
+
+    def own_relay():
+        return remote(own_slots(mx), own_slots(mx), of_send, of_recv, f, my)
+
+    def partial_field(k, b, whose):
+        direct = cross = None
+        nt = (((1,), (1,)), ((), ()))
+        for w in whose:
+            lhs = jnp.concatenate([held[k, w, r, b].reshape(R, LANES) for r in range(F)], axis=1)
+            starts = [
+                pl.multiple_of((lax.rem(f + r, F) * M + w) * LANES, LANES) for r in range(F)
+            ]
+            for c in range(2):
+                rhs = jnp.concatenate([maps[b, c, :, pl.ds(s, LANES)] for s in starts], axis=1)
+                term = lax.dot_general(lhs, rhs, nt, preferred_element_type=jnp.float32)
+                if c == 0:
+                    direct = term if direct is None else direct + term
+                else:
+                    cross = term if cross is None else cross + term
+        even = lax.rem(lax.broadcasted_iota(jnp.int32, (R, O), 0), 2) == 0
+        turned = jnp.where(even, -pltpu.roll(cross, R - 1, 0), pltpu.roll(cross, 1, 0))
+        return direct + turned
+
+    def near_part(k):
+        def one_bin(b, carry):
+            field[k, b] = partial_field(k, b, (m, mx, my)).reshape(F, C, O)
+            return carry
+
+        lax.fori_loop(0, B, one_bin, 0)
+
+    def far_part(k):
+        def one_bin(b, carry):
+            value = field[k, b].reshape(R, O) + partial_field(k, b, (md,))
+            field[k, b] = value.reshape(F, C, O)
+            root = (f * B + b + 1).astype(jnp.float32) / (B * F)
+            squares = jnp.sum((value * value).reshape(R // 8, 8, O), axis=0)
+            folded = squares[:, :LANES]
+            for j in range(1, O // LANES):
+                folded = folded + squares[:, j * LANES : (j + 1) * LANES]
+            power[...] += folded * (root * root)
+            return carry
+
+        lax.fori_loop(0, B, one_bin, 0)
+
+    def early_start(k):
+        early[f, k] = field[k, :, f]
+        for step in range(1, F):
+            there = freq_peer(step)
+            remote(
+                field.at[k, :, there], early.at[f, k], e_send.at[k], e_recv.at[k], there, m
+            ).start()
+
+    def early_slots(k):
+        return early.at[pl.ds(0, F - 1), k]
+
+    z_start(0)
+
+    def own_start(k, carry):
+        remote(chunk(f, k), held.at[k, m, 0], ox_send, ox_recv, f, mx).start()
+        remote(chunk(f, k), held.at[k, m, 0], oy_send, oy_recv, f, my).start()
+        own_copy(k).start()
+        return carry
+
+    lax.fori_loop(0, K, own_start, 0)
+    for k in range(1, min(AHEAD, K)):
+        z_start(k)
+    for b in range(B):
+        for c in range(2):
+            pltpu.make_async_copy(mapping.at[b, c], maps.at[b, c], map_sem.at[b, c]).start()
+    power[...] = jnp.zeros_like(power)
+
+    def step_fn(k, carry):
+        @pl.when(k < K)
+        def _():
+            await_bytes(z_slots(k), z_recv.at[k])
+            spread(k, m, mx, x_send, x_recv).start()
+            spread(k, m, my, y_send, y_recv).start()
+            own_copy(k).wait()
+
+        @pl.when(k + AHEAD < K)
+        def _():
+            z_start(k + AHEAD)
+
+        @pl.when(k == 0)
+        def _():
+            await_bytes(own_slots(mx), ox_recv)
+            own_relay().start()
+            await_bytes(own_slots(my), oy_recv)
+            for b in range(B):
+                for c in range(2):
+                    pltpu.make_async_copy(mapping.at[b, c], maps.at[b, c], map_sem.at[b, c]).wait()
+
+        @pl.when((k >= 1) & (k <= K))
+        def _():
+            last = k - 1
+            spread(last, mx, mx, x_send, x_recv).wait_recv()
+            relay_y(last).start()
+            spread(last, my, my, y_send, y_recv).wait_recv()
+            relay_x(last).start()
+            near_part(last)
+
+        @pl.when(k == 2)
+        def _():
+            own_relay().wait_recv()
+
+        @pl.when(k >= 2)
+        def _():
+            done = k - 2
+            relay_y(done).wait_recv()
+            relay_x(done).wait_recv()
+            far_part(done)
+
+            @pl.when(done < E)
+            def _():
+                early_start(done)
+
+        return carry
+
+    lax.fori_loop(0, K + 2, step_fn, 0)
+
+    by_mode[m] = power[...]
+    for step in range(1, M):
+        remote(power, by_mode.at[m], em_send, em_recv, f, mode_peer(step)).start()
+    await_bytes(by_mode.at[pl.ds(0, M - 1)], em_recv)
+    await_bytes(by_mode.at[pl.ds(0, M - 1)], em_send)
+    power[...] = jnp.sum(by_mode[...], axis=0)
+    by_freq[f] = power[...]
+    for step in range(1, F):
+        remote(power, by_freq.at[f], ef_send, ef_recv, freq_peer(step), m).start()
+    await_bytes(by_freq.at[pl.ds(0, F - 1)], ef_recv)
+    await_bytes(by_freq.at[pl.ds(0, F - 1)], ef_send)
+    count = F * K * C // 2 * O * M
+    energy = jnp.sum(jnp.sum(by_freq[...], axis=0), keepdims=True) / count
+    factor = jnp.sqrt(B * F / (energy + 1e-06))
+    blocks = O // LANES
+
+    def scale_late(d):
+        for k in range(E, K):
+            for b in range(B):
+                value = (field[k, b, d] * factor).astype(jnp.bfloat16)
+                for j in range(blocks):
+                    ready[d, b, j, (k - E) * C : (k - E + 1) * C] = value[:, j * LANES : (j + 1) * LANES]
+
+    def late_rows():
+        return out.at[pl.ds(f * B, B), :, pl.ds(E * C, (K - E) * C)]
+
+    def late_start(step, carry):
+        there = freq_peer(step)
+        scale_late(there)
+        remote(ready.at[there], late_rows(), o_send, o_recv, there, m).start()
+        return carry
+
+    lax.fori_loop(1, F, late_start, 0)
+    scale_late(f)
+    mine = pltpu.make_async_copy(ready.at[f], late_rows(), o_own.at[0])
+    mine.start()
+
+    def early_wait(k, carry):
+        await_bytes(early_slots(k), e_recv.at[k])
+        return carry
+
+    lax.fori_loop(0, E, early_wait, 0)
+
+    def scale_early(s, carry):
+        for k in range(E):
+            for b in range(B):
+                value = (early[s, k, b] * factor).astype(jnp.bfloat16)
+                for j in range(blocks):
+                    scaled[s * B + b, j, k * C : (k + 1) * C] = value[:, j * LANES : (j + 1) * LANES]
+        return carry
+
+    lax.fori_loop(0, F, scale_early, 0)
+    first = pltpu.make_async_copy(scaled, out.at[:, :, pl.ds(0, E * C)], o_own.at[1])
+    first.start()
+
+    def drain(k, carry):
+        await_bytes(z_slots(k), z_send.at[k])
+        spread(k, m, mx, x_send, x_recv).wait_send()
+        spread(k, m, my, y_send, y_recv).wait_send()
+        relay_y(k).wait_send()
+        relay_x(k).wait_send()
+
+        @pl.when(k < E)
+        def _():
+            await_bytes(early_slots(k), e_send.at[k])
+
+        return carry
+
+    lax.fori_loop(0, K, drain, 0)
+    await_bytes(own_slots(m), ox_send)
+    await_bytes(own_slots(m), oy_send)
+    own_relay().wait_send()
+    mine.wait()
+    first.wait()
+    await_bytes(ready.at[pl.ds(0, F - 1)], o_send)
+    await_bytes(ready.at[pl.ds(0, F - 1)], o_recv)
+
+
+def kernel_body(sources, mapping):
+    F = lax.axis_size("freq")
+    M = lax.axis_size("mode")
+    bins, snaps = sources.shape[:2]
+    B, _, O, modes = mapping.shape
+    rows = 2 * snaps // F
+    C = ROWS
+    K = rows // C
+    E = K * EARLY // 8
+    blocks = O // LANES
+    dma = pltpu.SemaphoreType.DMA
+    any_space = pl.BlockSpec(memory_space=pl.ANY)
+    out = pl.pallas_call(
+        functools.partial(kernel, (F, M, B, K, C, O, E)),
+        out_shape=jax.ShapeDtypeStruct((bins, blocks, rows, LANES), jnp.bfloat16),
+        in_specs=[any_space, any_space],
+        out_specs=any_space,
+        scratch_shapes=[
+            pltpu.VMEM((K, M, F, B, F, C, LANES), jnp.bfloat16),
+            pltpu.VMEM((B, 2, O, modes), jnp.bfloat16),
+            pltpu.VMEM((K, B, F, C, O), jnp.float32),
+            pltpu.VMEM((F, E, B, C, O), jnp.float32),
+            pltpu.VMEM((F, B, blocks, (K - E) * C, LANES), jnp.bfloat16),
+            pltpu.VMEM((bins, blocks, E * C, LANES), jnp.bfloat16),
+            pltpu.VMEM((8, LANES), jnp.float32),
+            pltpu.VMEM((M, 8, LANES), jnp.float32),
+            pltpu.VMEM((F, 8, LANES), jnp.float32),
+            dma((B, 2)),
+        ]
+        + [dma((K,))] * 11
+        + [dma((E,))] * 2
+        + [dma(())] * 10
+        + [dma((2,))]
+        + [dma(())] * 2,
+        compiler_params=pltpu.CompilerParams(
+            collective_id=0, has_side_effects=True, vmem_limit_bytes=62 * 1024 * 1024
+        ),
+    )(sources.reshape(bins, F, rows, LANES), mapping)
+    out = out.reshape(bins, blocks, rows // 2, 2, LANES)
+    return jnp.transpose(out, (0, 2, 3, 1, 4)).reshape(bins, rows // 2, 2, O)
+
+
+def body(sources, mapping):
+    freq_count = lax.axis_size("freq")
+    snaps, width = sources.shape[1], sources.shape[3]
+    held = 2 * mapping.size + 2 * mapping.shape[0] * snaps * 2 * mapping.shape[3]
+    fits = (
+        lax.axis_size("mode") == 4
+        and freq_count % 2 == 0
+        and width == LANES
+        and mapping.shape[2] % LANES == 0
+        and snaps % (4 * ROWS * freq_count) == 0
+        and held <= 40 * 1024 * 1024
+    )
+    return (kernel_body if fits else plain_body)(sources, mapping)
+
+
 def solution(mesh):
     placed = (P(None, None, None, ("freq", "mode")), P("freq", None, "mode", None))
     return jax.shard_map(

time: 474 us -> 190 us (0.40)
  blocking collectives: 186 us -> 0 us
  Pallas kernels: 0 us -> 185 us
  waiting for transfers between devices: 158 us -> 0 us
  local copies, waits for them, and re-layouts: 58.5 us -> 4.46 us
  matrix products: 46.6 us -> 0 us
  between operations: 14.2 us -> 0.01 us
  other arithmetic: 5.6 us -> 0 us
    pallas_call x0 -> x1, Pallas kernels: none -> 185 us  [kernel_body(): pl.pallas_call(functools.partial(kernel, (F, M, B, K, C, O, E)), out_shap...]
    all_gather x1 -> x0, waiting for transfers between devices: 158 us -> none  [body(): gathered = lax.all_gather(blocked, 'mode', axis=3, tiled=True)]
    all_to_all x2 -> x0, blocking collectives: 147 us -> none  [the longest x1 96.5 us: body(): lax.all_to_all(sources, 'freq', split_axis=0, concat_axis=3, tiled=True)]
    dot_general x4 -> x0, matrix products: 46.6 us -> none  [the longest x1 12.4 us: body(): jnp.einsum('bsm,bom->bso', complete[:, :, 1], mapping[:, 0], preferred_el...]
    psum x1 -> x0, blocking collectives: 39.1 us -> none  [body(): energy = lax.psum(local_energy, ('freq', 'mode'))]
    reshape x1, local copies, waits for them, and re-layouts: 27.7 us -> 4.46 us  [kernel_body(): return jnp.transpose(out, (0, 2, 3, 1, 4)).reshape(bins, rows // 2, 2, O)]
    transpose x1 -> x0, local copies, waits for them, and re-layouts: 22.3 us -> none  [body(): complete = jnp.swapaxes(gathered, 3, 4).reshape(bin_count, snapshots, 2, -1)]
  transfers between devices with their start and end apart: 1 -> 0, of which waited for: 1 -> 0; matrix products, arithmetic and copies ran while one was open for 0% -> 0% of each run, Pallas kernels for 0% -> 0%
where the time goes in v2:
time: 190 us; the launch traced here: 189 us
  Pallas kernels  185 us (97%)
  local copies, waits for them, and re-layouts  4.46 us (2%)
    pallas_call x1, Pallas kernels, kernel_body(): pl.pallas_call(functools.partial(kernel, (F, M, B, K, C, O, E)), out_shap...  185 us
    reshape x1, local copies, waits for them, and re-layouts, kernel_body(): return jnp.transpose(out, (0, 2, 3, 1, 4)).reshape(bins, rows // 2, 2, O)  4.46 us

profile of v2, /device:TPU:9, one launch (start us, length us, event | category | flops | bytes accessed | tf_op | source)
XLA Modules:
  0.0 189.4 jit_solution(3814004619996057192)
XLA Ops:
  0.0 184.9 %shard_map.28 = bf16[16,4,128,128]{3,2,1,0:T(8,128)(2,1)} custom-call(bf16[16,8,128,128]{3,2,1,0:T(8,128)(2,1)} %bitcast.9, bf16[2,2,512,4096]{3,2,1,0:T(8,128)(2,1)} %mapping.1), custom_call_target="tpu_custom_call" | custom-call | tf_op jit(solution)/shard_map/pallas_call | solution.py:330
  184.9 4.5 %copy.6 = bf16[16,4,64,1,2,128]{5,4,1,3,2,0:T(2,128)(2,1)} copy(bf16[16,4,64,1,2,128]{5,4,3,2,1,0:T(2,128)(2,1)} %bitcast.8) | data formatting | bytes 4194304 | tf_op jit(solution)/shard_map/reshape | solution.py:357

commit v3 on v2

--- a/solution.py
+++ b/solution.py
@@ -11,7 +11,7 @@
 LANES = 128
 AHEAD = 3
 ROWS = 16
-EARLY = 5
+EARLY = 6
 
 
 def plain_body(sources, mapping):
@@ -263,13 +263,14 @@
     def late_rows():
         return out.at[pl.ds(f * B, B), :, pl.ds(E * C, (K - E) * C)]
 
-    def late_start(step, carry):
+    def late_start(i, carry):
+        step = lax.rem(cut + (1 - 2 * lax.rem(i, 2)) * ((i + 1) // 2) + F, F)
         there = freq_peer(step)
         scale_late(there)
         remote(ready.at[there], late_rows(), o_send, o_recv, there, m).start()
         return carry
 
-    lax.fori_loop(1, F, late_start, 0)
+    lax.fori_loop(0, F - 1, late_start, 0)
     scale_late(f)
     mine = pltpu.make_async_copy(ready.at[f], late_rows(), o_own.at[0])
     mine.start()

time: 190 us -> 184 us (0.968)
  Pallas kernels: 185 us -> 179 us
    pallas_call x1, Pallas kernels: 185 us -> 179 us  [kernel_body(): pl.pallas_call(functools.partial(kernel, (F, M, B, K, C, O, E)), out_shap...]
where the time goes in v3:
time: 184 us
  Pallas kernels  179 us (97%)
  local copies, waits for them, and re-layouts  4.46 us (2%)
    pallas_call x1, Pallas kernels, kernel_body(): pl.pallas_call(functools.partial(kernel, (F, M, B, K, C, O, E)), out_shap...  179 us
    reshape x1, local copies, waits for them, and re-layouts, kernel_body(): return jnp.transpose(out, (0, 2, 3, 1, 4)).reshape(bins, rows // 2, 2, O)  4.46 us

profile of v3, /device:TPU:9, one launch (start us, length us, event | category | flops | bytes accessed | tf_op | source)
XLA Modules:
  0.0 183.8 jit_solution(8890804109146274970)
XLA Ops:
  0.0 179.3 %shard_map.28 = bf16[16,4,128,128]{3,2,1,0:T(8,128)(2,1)} custom-call(bf16[16,8,128,128]{3,2,1,0:T(8,128)(2,1)} %bitcast.9, bf16[2,2,512,4096]{3,2,1,0:T(8,128)(2,1)} %mapping.1), custom_call_target="tpu_custom_call" | custom-call | tf_op jit(solution)/shard_map/pallas_call | solution.py:331
  179.3 4.5 %copy.6 = bf16[16,4,64,1,2,128]{5,4,1,3,2,0:T(2,128)(2,1)} copy(bf16[16,4,64,1,2,128]{5,4,3,2,1,0:T(2,128)(2,1)} %bitcast.8) | data formatting | bytes 4194304 | tf_op jit(solution)/shard_map/reshape | solution.py:358
